TPU v7x, 512 devices: a whole 4x4x16 slice. The times are simulated.
512 devices in a mesh: row: 32 (over z, y_lo), col: 16 (over y_hi, x, core).
Axes of the slice: x: 4, y: 4 (y_hi: 2, y_lo: 2; y = y_hi * 2 + y_lo), z: 16, core: 2. Of those that a mesh axis runs over, the one named last changes fastest.
Arguments:
- atom_feats: bfloat16 [32768, 128], P(('row', 'col')), may hold values from -6 to 6
- key_starts: int32 [1024], P(('row', 'col')), may hold values from -64 to 32704, as said below
- atom_counts: int32 [2048], replicated, may hold values from 8 to 24, as said below
- atom_gain: float32 [128], replicated, may hold values from 0.1 to 1.9
- w_query: bfloat16 [128, 128], replicated, may hold values from -0.5 to 0.5
- w_key: bfloat16 [128, 128], replicated, may hold values from -0.5 to 0.5
- w_value: bfloat16 [128, 128], replicated, may hold values from -0.5 to 0.5
- w_out: bfloat16 [128, 128], replicated, may hold values from -0.5 to 0.5
- w_pool: bfloat16 [128, 384], replicated, may hold values from -0.5 to 0.5
- w_back: bfloat16 [384, 128], replicated, may hold values from -0.3125 to 0.3125
- pair_state: bfloat16 [2048, 2048, 128], P('row', 'col'), may hold values from -6 to 6
- w_left: bfloat16 [384, 32], replicated, may hold values from -0.3125 to 0.3125
- w_right: bfloat16 [384, 32], replicated, may hold values from -0.3125 to 0.3125
- w_outer: bfloat16 [32, 32, 128], replicated, may hold values from -0.1875 to 0.1875
- pair_gain: float32 [128], replicated, may hold values from 0.1 to 1.9
- w_gate: bfloat16 [128, 512], replicated, may hold values from -0.5 to 0.5
- w_lift: bfloat16 [128, 512], replicated, may hold values from -0.5 to 0.5
- w_drop: bfloat16 [512, 128], replicated, may hold values from -0.25 to 0.25
Outputs:
- atom_out: bfloat16 [32768, 128], P(('row', 'col'))
- token_single: bfloat16 [2048, 384], P(('row', 'col'))
- pair_out: bfloat16 [2048, 2048, 128], P('row', 'col')
Inputs may be any that keep to these rules, and one draw needn't show every extreme that they name: key_starts[b] = 32 * b - 64 + offset, with offset a whole number from 0 to 32; the offset is 0 for the first block and 32 for the last. `atom_counts`: the counts sum to 32768.
All inputs are finite; a program needn't handle non-finite values.
Results may differ from a plain program's by a relative error of at most 0.007.
Values may be sent and summed in bfloat16 or wider, within the bound.
A program may use at most 64 MiB of HBM per device.

v0:
```python
import math
import jax
import jax.numpy as jnp
from jax import lax
from jax.sharding import PartitionSpec as P

HEADS = 4
QB = 32
KW = 128
FEWEST = 8
EPSILON = 1e-05


def with_halo(block, sides, width):
    for axis, dim in sides:
        count = lax.axis_size(axis)
        forward = [(i, i + 1) for i in range(count - 1)]
        backward = [(target, source) for source, target in forward]
        low = lax.ppermute(
            lax.slice_in_dim(block, block.shape[dim] - width, None, axis=dim), axis, forward
        )
        high = lax.ppermute(lax.slice_in_dim(block, 0, width, axis=dim), axis, backward)
        block = jnp.concatenate([low, block, high], axis=dim)
    return block


def shifted(block, axis, distance):
    devices = range(lax.axis_size(axis))
    route = [(i - distance, i) for i in devices if i - distance in devices]
    return lax.ppermute(block, axis, route)


def layer_norm(values, gain):
    mean_value = jnp.mean(values, axis=-1, keepdims=True)
    centred = values - mean_value
    variance = jnp.mean(centred * centred, axis=-1, keepdims=True)
    return centred * lax.rsqrt(variance + EPSILON) * gain


def project(source, weight):
    return jnp.dot(source, weight, preferred_element_type=jnp.float32).astype(jnp.bfloat16)


def per_device(
    atom_feats,
    key_starts,
    atom_counts,
    atom_gain,
    w_query,
    w_key,
    w_value,
    w_out,
    w_pool,
    w_back,
    pair_state,
    w_left,
    w_right,
    w_outer,
    pair_gain,
    w_gate,
    w_lift,
    w_drop,
):
    atom_rows, atom_width = atom_feats.shape
    devices = lax.axis_size(("row", "col"))
    position = lax.axis_index(("row", "col"))
    total_atoms = atom_rows * devices
    total_tokens = atom_counts.shape[0]
    own_tokens = total_tokens // devices
    rim_width = KW // 2
    first_atom = position * atom_rows
    atom_float = atom_feats.astype(jnp.float32)
    normed = layer_norm(atom_float, atom_gain).astype(jnp.bfloat16)
    queries = project(normed, w_query)
    w_keyval = jnp.concatenate([w_key, w_value], axis=1)
    keyvals = project(normed, w_keyval)
    extended = with_halo(keyvals, ((("row", "col"), 0),), rim_width)
    local_starts = key_starts - first_atom + rim_width
    windows = jax.vmap(lambda first_row: lax.dynamic_slice_in_dim(extended, first_row, KW, 0))(
        local_starts
    )
    head_size = atom_width // HEADS
    blocks = atom_rows // QB
    query_blocks = queries.reshape(blocks, QB, HEADS, head_size)
    key_blocks = windows[:, :, :atom_width].reshape(blocks, KW, HEADS, head_size)
    value_blocks = windows[:, :, atom_width:].reshape(blocks, KW, HEADS, head_size)
    key_index = key_starts[:, None] + jnp.arange(KW, dtype=jnp.int32)[None, :]
    in_range = (key_index >= 0) & (key_index < total_atoms)
    scores = jnp.einsum(
        "bqhd,bkhd->bhqk", query_blocks, key_blocks, preferred_element_type=jnp.float32
    ) * head_size ** (-0.5)
    raised = jnp.where(in_range[:, None, None, :], jnp.exp(scores), 0.0)
    weights = (raised / jnp.sum(raised, axis=-1, keepdims=True)).astype(jnp.bfloat16)
    attended = (
        jnp.einsum("bhqk,bkhd->bqhd", weights, value_blocks, preferred_element_type=jnp.float32)
        .astype(jnp.bfloat16)
        .reshape(atom_rows, atom_width)
    )
    updated = (atom_float + jnp.dot(attended, w_out, preferred_element_type=jnp.float32)).astype(
        jnp.bfloat16
    )
    feature = jax.nn.relu(jnp.dot(updated, w_pool, preferred_element_type=jnp.float32)).astype(
        jnp.bfloat16
    )
    token_ends = jnp.cumsum(atom_counts, dtype=jnp.int32)
    atom_index = first_atom + jnp.arange(atom_rows, dtype=jnp.int32)
    token_of = jnp.sum((token_ends[None, :] <= atom_index[:, None]).astype(jnp.int32), axis=1)
    count_float = atom_counts.astype(jnp.float32)
    slots = atom_rows // FEWEST
    token_starts = token_ends - atom_counts
    base_token = jnp.sum((token_starts < first_atom).astype(jnp.int32))
    relative = token_of - base_token
    slot_range = jnp.arange(slots, dtype=jnp.int32)
    member = (relative[:, None] == slot_range[None, :]).astype(jnp.bfloat16)
    local_sums = jnp.einsum("as,ac->sc", member, feature, preferred_element_type=jnp.float32)
    carried = (relative < 0).astype(jnp.bfloat16)[None, :]
    edge_sum = jnp.dot(carried, feature, preferred_element_type=jnp.float32)
    from_next = shifted(edge_sum, ("row", "col"), -1)
    next_token = jnp.sum((token_ends <= first_atom + atom_rows).astype(jnp.int32))
    target = (slot_range == next_token - base_token).astype(jnp.float32)[:, None]
    pooled_slots = local_sums + target * from_next
    padded_counts = jnp.concatenate([count_float, jnp.ones((slots,), jnp.float32)])
    slot_counts = lax.dynamic_slice_in_dim(padded_counts, base_token, slots, 0)
    slot_single = (pooled_slots / slot_counts[:, None]).astype(jnp.bfloat16)
    owner = token_starts // atom_rows
    owner_first = jnp.searchsorted(token_starts, owner * atom_rows, side="left")
    row_of = owner * slots + jnp.arange(total_tokens, dtype=jnp.int32) - owner_first
    gathered = lax.all_gather(slot_single, ("row", "col"), axis=0, tiled=True)
    full_single = jnp.take(gathered, row_of, axis=0)
    left_all = project(full_single, w_left)
    right_all = project(full_single, w_right)
    back_all = project(full_single, w_back)
    token_single = lax.dynamic_slice_in_dim(full_single, position * own_tokens, own_tokens, 0)
    member_all = (token_of[:, None] == jnp.arange(total_tokens, dtype=jnp.int32)[None, :]).astype(
        jnp.bfloat16
    )
    lifted = jnp.dot(member_all, back_all, preferred_element_type=jnp.float32)
    atom_out = (updated.astype(jnp.float32) + lifted).astype(jnp.bfloat16)
    row_tokens, col_tokens, pair_width = pair_state.shape
    left_rows = lax.dynamic_slice_in_dim(
        left_all, lax.axis_index("row") * row_tokens, row_tokens, 0
    )
    right_cols = lax.dynamic_slice_in_dim(
        right_all, lax.axis_index("col") * col_tokens, col_tokens, 0
    )
    outer_table = jnp.einsum(
        "jb,abc->jac", right_cols, w_outer, preferred_element_type=jnp.float32
    ).astype(jnp.bfloat16)
    step_rows = math.gcd(row_tokens, 8)

    def pair_block(pieces):
        left_block, pair_piece = pieces
        outer_term = jnp.einsum(
            "ia,jac->ijc", left_block, outer_table, preferred_element_type=jnp.float32
        )
        summed = pair_piece.astype(jnp.float32) + outer_term
        normed_pair = layer_norm(summed, pair_gain).astype(jnp.bfloat16)
        gate_proj = jnp.einsum(
            "ijc,cf->ijf", normed_pair, w_gate, preferred_element_type=jnp.float32
        )
        lift_proj = jnp.einsum(
            "ijc,cf->ijf", normed_pair, w_lift, preferred_element_type=jnp.float32
        )
        hidden = (jax.nn.silu(gate_proj) * lift_proj).astype(jnp.bfloat16)
        return (
            summed + jnp.einsum("ijf,fc->ijc", hidden, w_drop, preferred_element_type=jnp.float32)
        ).astype(jnp.bfloat16)

    pair_out = lax.map(
        pair_block,
        (
            left_rows.reshape(-1, step_rows, left_rows.shape[1]),
            pair_state.reshape(-1, step_rows, col_tokens, pair_width),
        ),
    )
    return (atom_out, token_single, pair_out.reshape(row_tokens, col_tokens, pair_width))


def solution(mesh):
    in_specs = (
        P(("row", "col"), None),
        P(("row", "col")),
        P(),
        P(),
        P(),
        P(),
        P(),
        P(),
        P(),
        P(),
        P("row", "col", None),
        P(),
        P(),
        P(),
        P(),
        P(),
        P(),
        P(),
    )
    out_specs = (P(("row", "col"), None), P(("row", "col"), None), P("row", "col", None))
    return jax.shard_map(
        per_device, mesh=mesh, in_specs=in_specs, out_specs=out_specs, check_vma=False
    )
```

profile of v0, /device:TPU:64, one launch (start us, length us, event | category | flops | bytes accessed | tf_op | source)
XLA Modules:
  0.0 1076.9 jit_solution(7566077309387999252)
XLA Ops:
  7.2 0.9 convert_reduce_fusion.1
  8.1 0.9 fusion.29
  9.0 1.0 convolution_convert_fusion.3
  10.0 6.1 collective-permute-start.1
  16.1 1.9 collective-permute-start
  18.1 0.7 compare_and_fusion.1
  18.8 0.7 fusion.42
  19.5 1.0 reduce-window.9
  20.7 0.9 broadcast_multiply_fusion.1
  21.5 0.7 convert_reduce_fusion.2
  22.2 1.0 convolution_convert_fusion.4
  23.2 142.4 %while.37 = (s32[]{:T(128)}, u32[2048]{0:T(1024)S(1)}, u32[2048]{0:T(1024)S(1)}, s32[2048]{0:T(1024)S(1)}, s32[2048]{0:T(1024)S(1)}, /*index=5*/s32[]{:T(128)}, s32[]{:T(128)}, s32[]{}) while((s32[]{:T(128)}, u32[2048]{0:T(1024)S(1)}, u32[2048]{0:T(1024)S(1)}, s32[2048]{0:T(1024)S(1)}, s32[2048]{0:T(1024)S(1)}, ...), condition=%wide.region_7.8_spmd.clone, body=%wide.region_6.7_spmd.clone.sunk | while | flops 38916 | bytes 135277 | solution.py:126
  23.2 11.8 %gather_fusion = s32[2048]{0:T(1024)S(1)} fusion(s32[2048]{0:T(1024)S(1)} %get-tuple-element.368, u32[2048]{0:T(1024)S(1)} %broadcast_clamp_fusion.3), kind=kCustom, calls=%fused_computation.clone.clone.1 | custom fusion | bytes 24576 | tf_op jit(solution)/shard_map/jit(searchsorted)/jit(_searchsorted_scan_impl)/vmap(jit(_searchsorted_scan_impl))/while/body/eval_jaxpr/gather | solution.py:126
  35.1 11.8 %gather_fusion = s32[2048]{0:T(1024)S(1)} fusion(s32[2048]{0:T(1024)S(1)} %get-tuple-element.368, u32[2048]{0:T(1024)S(1)} %broadcast_clamp_fusion.3), kind=kCustom, calls=%fused_computation.clone.clone.1 | custom fusion | bytes 24576 | tf_op jit(solution)/shard_map/jit(searchsorted)/jit(_searchsorted_scan_impl)/vmap(jit(_searchsorted_scan_impl))/while/body/eval_jaxpr/gather | solution.py:126
  47.0 11.8 %gather_fusion = s32[2048]{0:T(1024)S(1)} fusion(s32[2048]{0:T(1024)S(1)} %get-tuple-element.368, u32[2048]{0:T(1024)S(1)} %broadcast_clamp_fusion.3), kind=kCustom, calls=%fused_computation.clone.clone.1 | custom fusion | bytes 24576 | tf_op jit(solution)/shard_map/jit(searchsorted)/jit(_searchsorted_scan_impl)/vmap(jit(_searchsorted_scan_impl))/while/body/eval_jaxpr/gather | solution.py:126
  58.9 11.8 %gather_fusion = s32[2048]{0:T(1024)S(1)} fusion(s32[2048]{0:T(1024)S(1)} %get-tuple-element.368, u32[2048]{0:T(1024)S(1)} %broadcast_clamp_fusion.3), kind=kCustom, calls=%fused_computation.clone.clone.1 | custom fusion | bytes 24576 | tf_op jit(solution)/shard_map/jit(searchsorted)/jit(_searchsorted_scan_impl)/vmap(jit(_searchsorted_scan_impl))/while/body/eval_jaxpr/gather | solution.py:126
  70.7 11.8 %gather_fusion = s32[2048]{0:T(1024)S(1)} fusion(s32[2048]{0:T(1024)S(1)} %get-tuple-element.368, u32[2048]{0:T(1024)S(1)} %broadcast_clamp_fusion.3), kind=kCustom, calls=%fused_computation.clone.clone.1 | custom fusion | bytes 24576 | tf_op jit(solution)/shard_map/jit(searchsorted)/jit(_searchsorted_scan_impl)/vmap(jit(_searchsorted_scan_impl))/while/body/eval_jaxpr/gather | solution.py:126
  82.6 11.8 %gather_fusion = s32[2048]{0:T(1024)S(1)} fusion(s32[2048]{0:T(1024)S(1)} %get-tuple-element.368, u32[2048]{0:T(1024)S(1)} %broadcast_clamp_fusion.3), kind=kCustom, calls=%fused_computation.clone.clone.1 | custom fusion | bytes 24576 | tf_op jit(solution)/shard_map/jit(searchsorted)/jit(_searchsorted_scan_impl)/vmap(jit(_searchsorted_scan_impl))/while/body/eval_jaxpr/gather | solution.py:126
  94.5 11.8 %gather_fusion = s32[2048]{0:T(1024)S(1)} fusion(s32[2048]{0:T(1024)S(1)} %get-tuple-element.368, u32[2048]{0:T(1024)S(1)} %broadcast_clamp_fusion.3), kind=kCustom, calls=%fused_computation.clone.clone.1 | custom fusion | bytes 24576 | tf_op jit(solution)/shard_map/jit(searchsorted)/jit(_searchsorted_scan_impl)/vmap(jit(_searchsorted_scan_impl))/while/body/eval_jaxpr/gather | solution.py:126
  106.3 11.8 %gather_fusion = s32[2048]{0:T(1024)S(1)} fusion(s32[2048]{0:T(1024)S(1)} %get-tuple-element.368, u32[2048]{0:T(1024)S(1)} %broadcast_clamp_fusion.3), kind=kCustom, calls=%fused_computation.clone.clone.1 | custom fusion | bytes 24576 | tf_op jit(solution)/shard_map/jit(searchsorted)/jit(_searchsorted_scan_impl)/vmap(jit(_searchsorted_scan_impl))/while/body/eval_jaxpr/gather | solution.py:126
  118.2 11.8 %gather_fusion = s32[2048]{0:T(1024)S(1)} fusion(s32[2048]{0:T(1024)S(1)} %get-tuple-element.368, u32[2048]{0:T(1024)S(1)} %broadcast_clamp_fusion.3), kind=kCustom, calls=%fused_computation.clone.clone.1 | custom fusion | bytes 24576 | tf_op jit(solution)/shard_map/jit(searchsorted)/jit(_searchsorted_scan_impl)/vmap(jit(_searchsorted_scan_impl))/while/body/eval_jaxpr/gather | solution.py:126
  130.1 11.8 %gather_fusion = s32[2048]{0:T(1024)S(1)} fusion(s32[2048]{0:T(1024)S(1)} %get-tuple-element.368, u32[2048]{0:T(1024)S(1)} %broadcast_clamp_fusion.3), kind=kCustom, calls=%fused_computation.clone.clone.1 | custom fusion | bytes 24576 | tf_op jit(solution)/shard_map/jit(searchsorted)/jit(_searchsorted_scan_impl)/vmap(jit(_searchsorted_scan_impl))/while/body/eval_jaxpr/gather | solution.py:126
  141.9 11.8 %gather_fusion = s32[2048]{0:T(1024)S(1)} fusion(s32[2048]{0:T(1024)S(1)} %get-tuple-element.368, u32[2048]{0:T(1024)S(1)} %broadcast_clamp_fusion.3), kind=kCustom, calls=%fused_computation.clone.clone.1 | custom fusion | bytes 24576 | tf_op jit(solution)/shard_map/jit(searchsorted)/jit(_searchsorted_scan_impl)/vmap(jit(_searchsorted_scan_impl))/while/body/eval_jaxpr/gather | solution.py:126
  153.8 11.8 %gather_fusion = s32[2048]{0:T(1024)S(1)} fusion(s32[2048]{0:T(1024)S(1)} %get-tuple-element.368, u32[2048]{0:T(1024)S(1)} %broadcast_clamp_fusion.3), kind=kCustom, calls=%fused_computation.clone.clone.1 | custom fusion | bytes 24576 | tf_op jit(solution)/shard_map/jit(searchsorted)/jit(_searchsorted_scan_impl)/vmap(jit(_searchsorted_scan_impl))/while/body/eval_jaxpr/gather | solution.py:126
  172.2 7.9 collective-permute-start.2
  180.2 1.2 collective-permute-done.2
  181.4 0.8 divide_convert_fusion.2
  182.3 835.3 %all-gather.2.cloned.1.call-done = bf16[4096,384]{1,0:T(8,128)(2,1)} async-done(((bf16[8,384]{1,0:T(8,128)(2,1)}), bf16[4096,384]{1,0:T(8,128)(2,1)}) %all-gather.2.cloned.1.call-update) | async-done | bytes 3145744 | tf_op jit(solution)/shard_map/all_gather | solution.py:128
  1017.6 9.5 gather_fusion.1
  1028.0 1.4 fusion.19
  1031.8 0.7 copy.50
  1032.6 37.5 %while.35 = (s32[]{:T(128)}, bf16[8,8,128,128]{3,2,1,0:T(8,128)(2,1)}, bf16[8,8,128,128]{3,2,1,0:T(8,128)(2,1)}, bf16[8,8,32]{2,1,0:T(8,128)(2,1)S(1)}, bf16[128...) while((s32[]{:T(128)}, ...), condition=%wide.region_13.14_spmd, body=%wide.region_10.13_spmd.sunk | while | flops 415761408 | bytes 12229241 | solution.py:169
  1032.6 1.0 constant_dynamic-slice_fusion.5
  1035.1 0.7 multiply_convert_fusion.5
  1035.8 0.7 fusion.93
  1036.5 0.7 copy_dynamic-update-slice_fusion.2
  1037.3 1.0 constant_dynamic-slice_fusion.5
  1039.8 0.7 multiply_convert_fusion.5
  1040.5 0.7 fusion.93
  1041.2 0.7 copy_dynamic-update-slice_fusion.2
  1042.0 1.0 constant_dynamic-slice_fusion.5
  1044.5 0.7 multiply_convert_fusion.5
  1045.2 0.7 fusion.93
  1045.9 0.7 copy_dynamic-update-slice_fusion.2
  1046.7 1.0 constant_dynamic-slice_fusion.5
  1049.2 0.7 multiply_convert_fusion.5
  1049.9 0.7 fusion.93
  1050.6 0.7 copy_dynamic-update-slice_fusion.2
  1051.3 1.0 constant_dynamic-slice_fusion.5
  1053.8 0.7 multiply_convert_fusion.5
  1054.6 0.7 fusion.93
  1055.3 0.7 copy_dynamic-update-slice_fusion.2
  1056.0 1.0 constant_dynamic-slice_fusion.5
  1058.5 0.7 multiply_convert_fusion.5
  1059.2 0.7 fusion.93
  1060.0 0.7 copy_dynamic-update-slice_fusion.2
  1060.7 1.0 constant_dynamic-slice_fusion.5
  1063.2 0.7 multiply_convert_fusion.5
  1063.9 0.7 fusion.93
  1064.6 0.7 copy_dynamic-update-slice_fusion.2
  1065.4 1.0 constant_dynamic-slice_fusion.5
  1067.9 0.7 multiply_convert_fusion.5
  1068.6 0.7 fusion.93
  1069.3 0.7 copy_dynamic-update-slice_fusion.2
  (165 shorter events, 19.4 us)
Async XLA Ops:
  7.2 1024.2 %copy-start = (bf16[32,32,128]{2,1,0:T(8,128)(2,1)S(1)}, bf16[32,32,128]{2,1,0:T(8,128)(2,1)}, u32[]{:S(2)}) copy-start(bf16[32,32,128]{2,1,0:T(8,128)(2,1)} %param.35) | copy-start | bytes 786436
  7.2 1010.4 %all-gather.2.cloned.1.call-start = ((), (), s32[]{:S(2)}) async-start(), calls=%async_computation | async-start | bytes 3151872 | tf_op jit(solution)/shard_map/all_gather | solution.py:128
  10.0 160.6 %collective-permute-start.1 = (bf16[64,256]{1,0:T(8,128)(2,1)S(1)}, bf16[64,256]{1,0:T(8,128)(2,1)S(1)}, u32[]{:S(2)}, u32[]{:S(2)}) collective-permute-start(bf16[64,256]{1,0:T(8,128)(2,1)S(1)} %convolution_convert_fusion.3), channel_id=1, source_target_pairs={{1,0},{2,1},{3,2},{4,3},{5,4},{6,5},{7,6},{8,7},{9,8},{10,9},{11,1... | collective-permute-start | bytes 98312 | tf_op jit(solution)/shard_map/ppermute | solution.py:22
  16.1 154.5 %collective-permute-start = (bf16[64,256]{1,0:T(8,128)(2,1)S(1)}, bf16[64,256]{1,0:T(8,128)(2,1)S(1)}, u32[]{:S(2)}, u32[]{:S(2)}) collective-permute-start(bf16[64,256]{1,0:T(8,128)(2,1)S(1)} %convolution_convert_fusion.3), channel_id=1, source_target_pairs={{0,1},{1,2},{2,3},{3,4},{4,5},{5,6},{6,7},{7,8},{8,9},{9,10},{10,1... | collective-permute-start | bytes 98312 | tf_op jit(solution)/shard_map/ppermute | solution.py:19
  165.6 6.2 copy-start.3
  165.6 6.2 copy-start.5
  165.7 6.3 copy-start.4
  172.2 9.1 collective-permute-start.2
  1027.1 0.9 copy-start.10
  1027.1 2.9 copy-start.6
  1028.0 2.6 copy-start.7
  1031.1 1.4 copy-start.1
  1031.2 1.4 copy-start.2
  1031.2 1.4 copy-start.8
  1031.2 1.4 copy-start.9
Sparse Core Ops, SparseCore 0:
  182.4 835.1 all-gather.1
where the time goes:
time: 1080 us
  waiting for transfers between devices  836 us (77%)
  local copies, waits for them, and re-layouts  168 us (16%)
  matrix products  24.3 us (2%)
  between operations  17.7 us (2%)
  starting transfers between devices  15.9 us (1%)
  other arithmetic  13.9 us (1%)
    all_gather x1, waiting for transfers between devices, per_device(): gathered = lax.all_gather(slot_single, ('row', 'col'), axis=0, tiled=True)  835 us
    gather x12, local copies, waits for them, and re-layouts, per_device(): owner_first = jnp.searchsorted(token_starts, owner * atom_rows, side='left')  141 us
  transfers between devices with their start and end apart: 4, of which 2 were waited for; matrix products, arithmetic and copies ran while one was open for 14% of the time, Pallas kernels for 0%

commit v1 on v0

--- a/solution.py
+++ b/solution.py
@@ -9,6 +9,13 @@
 KW = 128
 FEWEST = 8
 EPSILON = 1e-05
+
+
+def swapped_in(x, axis, along):
+    peers = lax.axis_size(axis)
+    shards = jnp.stack([x for _ in range(peers)])
+    shards = lax.all_to_all(shards, axis, split_axis=0, concat_axis=0)
+    return jnp.concatenate(shards, axis=along)
 
 
 def with_halo(block, sides, width):
@@ -125,7 +132,7 @@
     owner = token_starts // atom_rows
     owner_first = jnp.searchsorted(token_starts, owner * atom_rows, side="left")
     row_of = owner * slots + jnp.arange(total_tokens, dtype=jnp.int32) - owner_first
-    gathered = lax.all_gather(slot_single, ("row", "col"), axis=0, tiled=True)
+    gathered = swapped_in(slot_single, ("row", "col"), 0)
     full_single = jnp.take(gathered, row_of, axis=0)
     left_all = project(full_single, w_left)
     right_all = project(full_single, w_right)

time: 1080 us -> 402 us (0.37)
  the two profiles are of different devices: /device:TPU:64 before, /device:TPU:1 now
where the time goes in v1:
time: 402 us
  local copies, waits for them, and re-layouts  169 us (42%)
  waiting for transfers between devices  149 us (37%)
  starting transfers between devices  40.8 us (10%)
  matrix products  22.9 us (6%)
  other arithmetic  15.1 us (4%)
  between operations  4.29 us (1%)
    all_to_all x1, waiting for transfers between devices, swapped_in(): shards = lax.all_to_all(shards, axis, split_axis=0, concat_axis=0)  146 us
    gather x12, local copies, waits for them, and re-layouts, per_device(): owner_first = jnp.searchsorted(token_starts, owner * atom_rows, side='left')  141 us
    all_to_all x1, starting transfers between devices, swapped_in(): shards = lax.all_to_all(shards, axis, split_axis=0, concat_axis=0)  27.7 us
    gather x1, local copies, waits for them, and re-layouts, per_device(): full_single = jnp.take(gathered, row_of, axis=0)  9.04 us
    ppermute x1, starting transfers between devices, with_halo(): lax.ppermute(lax.slice_in_dim(block, 0, width, axis=dim), axis, backward)  8.75 us
  transfers between devices with their start and end apart: 4, of which 2 were waited for; matrix products, arithmetic and copies ran while one was open for 37% of the time, Pallas kernels for 0%

profile of v1, /device:TPU:1, one launch (start us, length us, event | category | flops | bytes accessed | tf_op | source)
XLA Modules:
  0.0 401.6 jit_solution(13150332468949652769)
XLA Ops:
  0.6 0.9 convert_reduce_fusion.1
  1.5 0.9 fusion.29
  2.4 1.0 convolution_convert_fusion.3
  3.5 8.7 %collective-permute-start.1 = (bf16[64,256]{1,0:T(8,128)(2,1)S(1)}, bf16[64,256]{1,0:T(8,128)(2,1)S(1)}, u32[]{:S(2)}, u32[]{:S(2)}) collective-permute-start(bf16[64,256]{1,0:T(8,128)(2,1)S(1)} %convolution_convert_fusion.3), channel_id=1, source_target_pairs={{1,0},{2,1},{3,2},{4,3},{5,4},{6,5},{7,6},{8,7},{9,8},{10,9},{11,1... | collective-permute-start | bytes 98312 | tf_op jit(solution)/shard_map/ppermute | solution.py:29
  12.2 1.9 collective-permute-start
  14.2 0.7 compare_and_fusion.1
  15.6 1.0 reduce-window.9
  16.8 0.9 broadcast_multiply_fusion.1
  17.7 142.4 %while.37 = (s32[]{:T(128)}, u32[2048]{0:T(1024)S(1)}, u32[2048]{0:T(1024)S(1)}, s32[2048]{0:T(1024)S(1)}, s32[2048]{0:T(1024)S(1)}, /*index=5*/s32[]{:T(128)}, s32[]{:T(128)}, s32[]{}) while((s32[]{:T(128)}, u32[2048]{0:T(1024)S(1)}, u32[2048]{0:T(1024)S(1)}, s32[2048]{0:T(1024)S(1)}, s32[2048]{0:T(1024)S(1)}, ...), condition=%wide.region_7.8_spmd.clone, body=%wide.region_6.7_spmd.clone.sunk | while | flops 38916 | bytes 135285 | solution.py:133
  17.7 11.8 %gather_fusion = s32[2048]{0:T(1024)S(1)} fusion(s32[2048]{0:T(1024)S(1)} %get-tuple-element.368, u32[2048]{0:T(1024)S(1)} %broadcast_clamp_fusion.3), kind=kCustom, calls=%fused_computation.clone.clone.1 | custom fusion | bytes 24576 | tf_op jit(solution)/shard_map/jit(searchsorted)/jit(_searchsorted_scan_impl)/vmap(jit(_searchsorted_scan_impl))/while/body/eval_jaxpr/gather | solution.py:133
  29.6 11.8 %gather_fusion = s32[2048]{0:T(1024)S(1)} fusion(s32[2048]{0:T(1024)S(1)} %get-tuple-element.368, u32[2048]{0:T(1024)S(1)} %broadcast_clamp_fusion.3), kind=kCustom, calls=%fused_computation.clone.clone.1 | custom fusion | bytes 24576 | tf_op jit(solution)/shard_map/jit(searchsorted)/jit(_searchsorted_scan_impl)/vmap(jit(_searchsorted_scan_impl))/while/body/eval_jaxpr/gather | solution.py:133
  41.4 11.8 %gather_fusion = s32[2048]{0:T(1024)S(1)} fusion(s32[2048]{0:T(1024)S(1)} %get-tuple-element.368, u32[2048]{0:T(1024)S(1)} %broadcast_clamp_fusion.3), kind=kCustom, calls=%fused_computation.clone.clone.1 | custom fusion | bytes 24576 | tf_op jit(solution)/shard_map/jit(searchsorted)/jit(_searchsorted_scan_impl)/vmap(jit(_searchsorted_scan_impl))/while/body/eval_jaxpr/gather | solution.py:133
  53.3 11.8 %gather_fusion = s32[2048]{0:T(1024)S(1)} fusion(s32[2048]{0:T(1024)S(1)} %get-tuple-element.368, u32[2048]{0:T(1024)S(1)} %broadcast_clamp_fusion.3), kind=kCustom, calls=%fused_computation.clone.clone.1 | custom fusion | bytes 24576 | tf_op jit(solution)/shard_map/jit(searchsorted)/jit(_searchsorted_scan_impl)/vmap(jit(_searchsorted_scan_impl))/while/body/eval_jaxpr/gather | solution.py:133
  65.2 11.8 %gather_fusion = s32[2048]{0:T(1024)S(1)} fusion(s32[2048]{0:T(1024)S(1)} %get-tuple-element.368, u32[2048]{0:T(1024)S(1)} %broadcast_clamp_fusion.3), kind=kCustom, calls=%fused_computation.clone.clone.1 | custom fusion | bytes 24576 | tf_op jit(solution)/shard_map/jit(searchsorted)/jit(_searchsorted_scan_impl)/vmap(jit(_searchsorted_scan_impl))/while/body/eval_jaxpr/gather | solution.py:133
  77.0 11.8 %gather_fusion = s32[2048]{0:T(1024)S(1)} fusion(s32[2048]{0:T(1024)S(1)} %get-tuple-element.368, u32[2048]{0:T(1024)S(1)} %broadcast_clamp_fusion.3), kind=kCustom, calls=%fused_computation.clone.clone.1 | custom fusion | bytes 24576 | tf_op jit(solution)/shard_map/jit(searchsorted)/jit(_searchsorted_scan_impl)/vmap(jit(_searchsorted_scan_impl))/while/body/eval_jaxpr/gather | solution.py:133
  88.9 11.8 %gather_fusion = s32[2048]{0:T(1024)S(1)} fusion(s32[2048]{0:T(1024)S(1)} %get-tuple-element.368, u32[2048]{0:T(1024)S(1)} %broadcast_clamp_fusion.3), kind=kCustom, calls=%fused_computation.clone.clone.1 | custom fusion | bytes 24576 | tf_op jit(solution)/shard_map/jit(searchsorted)/jit(_searchsorted_scan_impl)/vmap(jit(_searchsorted_scan_impl))/while/body/eval_jaxpr/gather | solution.py:133
  100.8 11.8 %gather_fusion = s32[2048]{0:T(1024)S(1)} fusion(s32[2048]{0:T(1024)S(1)} %get-tuple-element.368, u32[2048]{0:T(1024)S(1)} %broadcast_clamp_fusion.3), kind=kCustom, calls=%fused_computation.clone.clone.1 | custom fusion | bytes 24576 | tf_op jit(solution)/shard_map/jit(searchsorted)/jit(_searchsorted_scan_impl)/vmap(jit(_searchsorted_scan_impl))/while/body/eval_jaxpr/gather | solution.py:133
  112.6 11.8 %gather_fusion = s32[2048]{0:T(1024)S(1)} fusion(s32[2048]{0:T(1024)S(1)} %get-tuple-element.368, u32[2048]{0:T(1024)S(1)} %broadcast_clamp_fusion.3), kind=kCustom, calls=%fused_computation.clone.clone.1 | custom fusion | bytes 24576 | tf_op jit(solution)/shard_map/jit(searchsorted)/jit(_searchsorted_scan_impl)/vmap(jit(_searchsorted_scan_impl))/while/body/eval_jaxpr/gather | solution.py:133
  124.5 11.8 %gather_fusion = s32[2048]{0:T(1024)S(1)} fusion(s32[2048]{0:T(1024)S(1)} %get-tuple-element.368, u32[2048]{0:T(1024)S(1)} %broadcast_clamp_fusion.3), kind=kCustom, calls=%fused_computation.clone.clone.1 | custom fusion | bytes 24576 | tf_op jit(solution)/shard_map/jit(searchsorted)/jit(_searchsorted_scan_impl)/vmap(jit(_searchsorted_scan_impl))/while/body/eval_jaxpr/gather | solution.py:133
  136.4 11.8 %gather_fusion = s32[2048]{0:T(1024)S(1)} fusion(s32[2048]{0:T(1024)S(1)} %get-tuple-element.368, u32[2048]{0:T(1024)S(1)} %broadcast_clamp_fusion.3), kind=kCustom, calls=%fused_computation.clone.clone.1 | custom fusion | bytes 24576 | tf_op jit(solution)/shard_map/jit(searchsorted)/jit(_searchsorted_scan_impl)/vmap(jit(_searchsorted_scan_impl))/while/body/eval_jaxpr/gather | solution.py:133
  148.2 11.8 %gather_fusion = s32[2048]{0:T(1024)S(1)} fusion(s32[2048]{0:T(1024)S(1)} %get-tuple-element.368, u32[2048]{0:T(1024)S(1)} %broadcast_clamp_fusion.3), kind=kCustom, calls=%fused_computation.clone.clone.1 | custom fusion | bytes 24576 | tf_op jit(solution)/shard_map/jit(searchsorted)/jit(_searchsorted_scan_impl)/vmap(jit(_searchsorted_scan_impl))/while/body/eval_jaxpr/gather | solution.py:133
  160.9 0.7 convert_reduce_fusion.2
  167.6 2.4 collective-permute-start.2
  170.1 2.4 collective-permute-done.2
  172.7 1.9 stack.2
  174.7 27.7 %all-to-all-start = ((bf16[512,8,384]{2,1,0:T(8,128)(2,1)}), bf16[512,8,384]{2,1,0:T(8,128)(2,1)S(1)}, u32[]{:S(2)}, u32[]{:S(2)}) async-start(bf16[512,8,384]{2,1,0:T(8,128)(2,1)} %stack.2), calls=%async_computation | async-start | bytes 6291456 | tf_op jit(solution)/shard_map/all_to_all | solution.py:17
  202.4 146.4 %all-to-all-done = bf16[512,8,384]{2,1,0:T(8,128)(2,1)S(1)} async-done(((bf16[512,8,384]{2,1,0:T(8,128)(2,1)}), bf16[512,8,384]{2,1,0:T(8,128)(2,1)S(1)}, u32[]{:S(2)}, u32[]{:S(2)}) %all-to-all-start) | async-done | bytes 3145760 | tf_op jit(solution)/shard_map/all_to_all | solution.py:17
  348.8 9.0 %gather_fusion.1 = bf16[2048,384]{1,0:T(8,128)(2,1)} fusion(bf16[4096,384]{1,0:T(8,128)(2,1)S(1)} %bitcast.82, s32[2048]{0:T(1024)S(1)} %get-tuple-element.227), kind=kCustom, calls=%fused_computation.1 | custom fusion | bytes 3153920 | tf_op jit(solution)/shard_map/jit(_take)/gather | solution.py:136
  357.8 1.6 broadcast_select_fusion
  359.5 1.4 fusion.19
  363.4 0.7 copy.50
  364.1 37.5 %while.35 = (s32[]{:T(128)}, bf16[8,8,128,128]{3,2,1,0:T(8,128)(2,1)}, bf16[8,8,128,128]{3,2,1,0:T(8,128)(2,1)}, bf16[8,8,32]{2,1,0:T(8,128)(2,1)S(1)}, bf16[128...) while((s32[]{:T(128)}, ...), condition=%wide.region_13.14_spmd, body=%wide.region_10.13_spmd.sunk | while | flops 415761408 | bytes 12229241 | solution.py:176
  364.1 1.0 constant_dynamic-slice_fusion.5
  366.6 0.7 multiply_convert_fusion.5
  367.4 0.7 fusion.93
  368.1 0.7 copy_dynamic-update-slice_fusion.2
  368.8 1.0 constant_dynamic-slice_fusion.5
  371.3 0.7 multiply_convert_fusion.5
  372.1 0.7 fusion.93
  372.8 0.7 copy_dynamic-update-slice_fusion.2
  373.5 1.0 constant_dynamic-slice_fusion.5
  376.0 0.7 multiply_convert_fusion.5
  376.7 0.7 fusion.93
  377.5 0.7 copy_dynamic-update-slice_fusion.2
  378.2 1.0 constant_dynamic-slice_fusion.5
  380.7 0.7 multiply_convert_fusion.5
  381.4 0.7 fusion.93
  382.1 0.7 copy_dynamic-update-slice_fusion.2
  382.9 1.0 constant_dynamic-slice_fusion.5
  385.4 0.7 multiply_convert_fusion.5
  386.1 0.7 fusion.93
  386.8 0.7 copy_dynamic-update-slice_fusion.2
  387.6 1.0 constant_dynamic-slice_fusion.5
  390.1 0.7 multiply_convert_fusion.5
  390.8 0.7 fusion.93
  391.5 0.7 copy_dynamic-update-slice_fusion.2
  392.3 1.0 constant_dynamic-slice_fusion.5
  394.7 0.7 multiply_convert_fusion.5
  395.5 0.7 fusion.93
  396.2 0.7 copy_dynamic-update-slice_fusion.2
  396.9 1.0 constant_dynamic-slice_fusion.5
  399.4 0.7 multiply_convert_fusion.5
  400.1 0.7 fusion.93
  400.9 0.7 copy_dynamic-update-slice_fusion.2
  (169 shorter events, 19.6 us)
Async XLA Ops:
  0.6 362.2 %copy-start = (bf16[32,32,128]{2,1,0:T(8,128)(2,1)S(1)}, bf16[32,32,128]{2,1,0:T(8,128)(2,1)}, u32[]{:S(2)}) copy-start(bf16[32,32,128]{2,1,0:T(8,128)(2,1)} %param.35) | copy-start | bytes 786436
  3.5 162.5 %collective-permute-start.1 = (bf16[64,256]{1,0:T(8,128)(2,1)S(1)}, bf16[64,256]{1,0:T(8,128)(2,1)S(1)}, u32[]{:S(2)}, u32[]{:S(2)}) collective-permute-start(bf16[64,256]{1,0:T(8,128)(2,1)S(1)} %convolution_convert_fusion.3), channel_id=1, source_target_pairs={{1,0},{2,1},{3,2},{4,3},{5,4},{6,5},{7,6},{8,7},{9,8},{10,9},{11,1... | collective-permute-start | bytes 98312 | tf_op jit(solution)/shard_map/ppermute | solution.py:29
  12.2 153.8 %collective-permute-start = (bf16[64,256]{1,0:T(8,128)(2,1)S(1)}, bf16[64,256]{1,0:T(8,128)(2,1)S(1)}, u32[]{:S(2)}, u32[]{:S(2)}) collective-permute-start(bf16[64,256]{1,0:T(8,128)(2,1)S(1)} %convolution_convert_fusion.3), channel_id=1, source_target_pairs={{0,1},{1,2},{2,3},{3,4},{4,5},{5,6},{6,7},{7,8},{8,9},{9,10},{10,1... | collective-permute-start | bytes 98312 | tf_op jit(solution)/shard_map/ppermute | solution.py:26
  17.6 143.1 %copy-start.3 = (bf16[64,128]{1,0:T(8,128)(2,1)S(1)}, bf16[64,128]{1,0:T(8,128)(2,1)}, u32[]{:S(2)}) copy-start(bf16[64,128]{1,0:T(8,128)(2,1)} %param.22) | copy-start | bytes 49156
  17.6 143.1 %copy-start.11 = (bf16[128,128]{1,0:T(8,128)(2,1)S(1)}, bf16[128,128]{1,0:T(8,128)(2,1)}, u32[]{:S(2)}) copy-start(bf16[128,128]{1,0:T(8,128)(2,1)} %param.26) | copy-start | bytes 98308
  17.6 143.1 %copy-start.12 = (f32[128]{0:T(128)S(1)}, f32[128]{0:T(128)}, u32[]{:S(2)}) copy-start(f32[128]{0:T(128)} %param.25) | copy-start | bytes 1540
  160.1 7.1 %copy-start.5 = (bf16[128,128]{1,0:T(8,128)(2,1)S(1)}, bf16[128,128]{1,0:T(8,128)(2,1)}, u32[]{:S(2)}) copy-start(bf16[128,128]{1,0:T(8,128)(2,1)} %param.29) | copy-start | bytes 98308
  160.1 7.2 %copy-start.4 = (bf16[128,384]{1,0:T(8,128)(2,1)S(1)}, bf16[128,384]{1,0:T(8,128)(2,1)}, u32[]{:S(2)}) copy-start(bf16[128,384]{1,0:T(8,128)(2,1)} %param.30) | copy-start | bytes 294916
  167.6 4.9 %collective-permute-start.2 = (f32[1,384]{1,0:T(1,128)S(1)}, f32[1,384]{1,0:T(1,128)S(1)}, u32[]{:S(2)}, u32[]{:S(2)}) collective-permute-start(f32[1,384]{1,0:T(1,128)S(1)} %fusion.38), channel_id=1, source_target_pairs={{1,0},{2,1},{3,2},{4,3},{5,4},{6,5},{7,6},{8,7},{9,8},{10,9},{11,1... | collective-permute-start | bytes 4616 | tf_op jit(solution)/shard_map/ppermute | solution.py:37
  174.7 174.1 %all-to-all-start = ((bf16[512,8,384]{2,1,0:T(8,128)(2,1)}), bf16[512,8,384]{2,1,0:T(8,128)(2,1)S(1)}, u32[]{:S(2)}, u32[]{:S(2)}) async-start(bf16[512,8,384]{2,1,0:T(8,128)(2,1)} %stack.2), calls=%async_computation | async-start | bytes 6291456 | tf_op jit(solution)/shard_map/all_to_all | solution.py:17
  357.8 1.6 copy-start.10
  357.8 3.7 copy-start.6
  359.5 2.8 copy-start.7
  362.9 1.2 copy-start.1
  362.9 1.2 copy-start.2
  362.9 1.2 copy-start.8
  362.9 1.2 copy-start.9
